TPU v7x, 32 devices: a whole 2x2x4 slice. The times are simulated.
32 devices in a mesh: rows: 8 (over y, x, core), grp: 4 (over z).
Axes of the slice: x: 2, y: 2, z: 4, core: 2. Of those that a mesh axis runs over, the one named last changes fastest.
Arguments:
- date_keys: int32 [262144], P(('rows', 'grp')), may hold values from 0 to 2559
- product_keys: int32 [262144], P(('rows', 'grp')), may hold values from 0 to 16255
- quantity: float32 [262144], P(('rows', 'grp')), may hold values from 0.01 to 10
- date_flags: int32 [2560], P('rows'), may hold values 0 or 1
- category: int32 [16256], P('rows'), may hold values from 0 to 999
- unit_price: float32 [16256], P('rows'), may hold values from 0.5 to 4
- unit_cost: float32 [16256], P('rows'), may hold values from 0.25 to 2
Outputs:
- revenue_by_category: float32 [1000], replicated
- profit_by_category: float32 [1000], replicated
All inputs are finite; a program needn't handle non-finite values. No bound on the sum of `date_flags` on one device may be relied on, other than what follows from the above.
Results may differ from a plain program's by a relative error of at most 0.00005.
Values sent between devices are 32-bit elements; how exact they have to be, the bound alone decides.
A program may use at most 192 MiB of HBM per device.

v0:
```python
import jax
import jax.numpy as jnp
from jax import lax
from jax.sharding import PartitionSpec as P

CATS = 1000


def category_sums(group_ids, amounts):
    length = group_ids.shape[0]
    padded = (CATS + 127) // 128 * 128
    block_rows = min(2048, (length + 127) // 128 * 128)
    total_rows = (length + block_rows - 1) // block_rows * block_rows
    extra = total_rows - length
    group_ids = jnp.concatenate([group_ids, jnp.full((extra,), padded, jnp.int32)])
    amounts = jnp.concatenate([amounts, jnp.zeros((2, extra), jnp.float32)], axis=1)
    columns = lax.broadcasted_iota(jnp.int32, (block_rows, padded), 1)

    def add_block(running, pieces):
        block_ids, block_amounts = pieces
        onehot = (block_ids[:, None] == columns).astype(jnp.float32)
        summed = jnp.dot(
            block_amounts,
            onehot,
            precision=lax.Precision.HIGHEST,
            preferred_element_type=jnp.float32,
        )
        return (running + summed, None)

    stacked = amounts.reshape(2, total_rows // block_rows, block_rows).transpose(1, 0, 2)
    running, _ = lax.scan(
        add_block, jnp.zeros((2, padded), jnp.float32), (group_ids.reshape(-1, block_rows), stacked)
    )
    return running


def window_sums(product_keys, kept_amount, row_count):
    inside = (product_keys >= 0) & (product_keys < row_count)
    segment = jnp.where(inside, product_keys, row_count)
    summed = jax.ops.segment_sum(
        jnp.where(inside, kept_amount, 0.0), segment, num_segments=row_count + 1
    )
    return summed[:row_count]


def body(date_keys, product_keys, quantity, date_flags, category, unit_price, unit_cost):
    date_mask = lax.all_gather(date_flags, "rows", axis=0, tiled=True)
    passed = jnp.take(date_mask, date_keys, axis=0)
    kept_amount = jnp.where(passed == 1, quantity, 0.0)
    shard_len = unit_price.shape[0]
    amount = lax.psum_scatter(
        window_sums(product_keys, kept_amount, shard_len * lax.axis_size("rows")),
        "rows",
        scatter_dimension=0,
        tiled=True,
    )
    revenue = amount * unit_price
    profit = amount * (unit_price - unit_cost)
    partial_value = category_sums(category, jnp.stack([revenue, profit]))
    totals = lax.psum(partial_value, ("rows", "grp"))
    fact_total = date_keys.shape[0] * lax.axis_size("rows") * lax.axis_size("grp")
    factor = CATS / fact_total
    return (totals[0, :CATS] * factor, totals[1, :CATS] * factor)


def solution(mesh):
    return jax.shard_map(
        body,
        mesh=mesh,
        in_specs=(
            P(("rows", "grp")),
            P(("rows", "grp")),
            P(("rows", "grp")),
            P("rows"),
            P("rows"),
            P("rows"),
            P("rows"),
        ),
        out_specs=(P(), P()),
        check_vma=False,
    )
```

profile of v0, /device:TPU:0, one launch (start us, length us, event | category | flops | bytes accessed | tf_op | source)
XLA Modules:
  0.0 184.5 jit_solution(4197366333144670196)
XLA Ops:
  0.6 0.0 copy-start
  0.7 1.3 fusion.16
  2.6 0.9 dynamic-update-slice
  3.5 25.5 %all-reduce.2 = s32[2560]{0:T(1024)S(1)} all-reduce(s32[2560]{0:T(1024)S(1)} %dynamic-update-slice), channel_id=1, replica_groups=mesh['rows'=8,'grp'=4] {'rows'}, use_global_device_ids=true, to_apply=%add.2 | all-reduce | flops 2560 | bytes 20480
  29.1 0.0 copy-done
  29.1 0.0 copy-start.1
  29.1 0.0 copy-start.2
  29.1 45.5 %gather_fusion = s32[8192]{0:T(1024)S(1)} fusion(s32[2560]{0:T(1024)S(1)} %all-reduce.2, s32[8192]{0:T(1024)S(1)} %fusion.4), kind=kCustom, calls=%fused_computation | custom fusion | bytes 98304 | tf_op jit(solution)/shard_map/jit(_take)/gather | solution.py:48
  74.6 0.0 copy-done.1
  74.7 0.0 copy-done.2
  74.7 43.2 %scatter_custom_fusion = f32[16257]{0:T(1024)S(1)} fusion(s32[8192]{0:T(1024)S(1)} %fusion.5, f32[8192]{0:T(1024)S(1)} %select_select_fusion, f32[]{:T(128)} %constant.10.clone.1), kind=kCustom, calls=%fused_computation.8 | custom fusion | flops 8192 | bytes 65032 | tf_op jit(solution)/shard_map/scatter-add | solution.py:40
  117.9 0.0 copy-start.4
  118.0 0.0 copy-start.5
  118.0 0.0 copy-start.3
  118.0 22.9 %all-reduce.3 = f32[16256]{0:T(1024)S(1)} all-reduce(f32[16256]{0:T(1024)S(1)} %bitcast.7), channel_id=2, replica_groups=mesh['rows'=8,'grp'=4] {'rows'}, use_global_device_ids=true, to_apply=%region_1.2.clone | all-reduce | flops 16256 | bytes 130048
  141.5 0.0 copy-done.4
  141.5 0.0 copy-done.5
  141.5 0.1 dynamic-slice_multiply_fusion
  141.6 0.0 copy-done.3
  141.6 2.7 %fusion = f32[2,1024]{1,0:T(2,128)S(1)} fusion(s32[2048]{0:T(1024)S(1)} %concatenate.7, f32[1,2032]{1,0:T(1,128)S(1)} %bitcast.9, f32[1,2032]{1,0:T(1,128)S(1)} %bitcast.8), kind=kOutput, calls=%fused_computation.3 | convolution fusion | flops 52445184 | bytes 32640 | tf_op jit(solution)/shard_map/while/body/eval_jaxpr/dot_general | solution.py:22
  144.4 39.5 %psum.7 = f32[2,1024]{1,0:T(2,128)S(1)} all-reduce(f32[2,1024]{1,0:T(2,128)S(1)} %fusion), channel_id=1, replica_groups=mesh['rows'=8,'grp'=4] {'rows','grp'}, use_global_device_ids=true, to_apply=%region_2.3 | all-reduce | flops 2048 | bytes 16384 | tf_op jit(solution)/shard_map/psum | solution.py:60
  183.9 0.6 slice_multiply_fusion
  (5 shorter events, 0.0 us)
Async XLA Ops:
  0.6 28.4 %copy-start = (s32[8192]{0:T(1024)S(1)}, s32[8192]{0:T(1024)}, u32[]{:S(2)}) copy-start(s32[8192]{0:T(1024)} %param.7) | copy-start | bytes 98308
  29.1 45.6 %copy-start.1 = (s32[8192]{0:T(1024)S(1)}, s32[8192]{0:T(1024)}, u32[]{:S(2)}) copy-start(s32[8192]{0:T(1024)} %param.8) | copy-start | bytes 98308
  29.1 45.6 %copy-start.2 = (f32[8192]{0:T(1024)S(1)}, f32[8192]{0:T(1024)}, u32[]{:S(2)}) copy-start(f32[8192]{0:T(1024)} %param.9) | copy-start | bytes 98308
  117.9 23.6 %copy-start.4 = (f32[2032]{0:T(1024)S(1)}, f32[2032]{0:T(1024)}, u32[]{:S(2)}) copy-start(f32[2032]{0:T(1024)} %param.12) | copy-start | bytes 24388
  118.0 23.6 %copy-start.5 = (f32[2032]{0:T(1024)S(1)}, f32[2032]{0:T(1024)}, u32[]{:S(2)}) copy-start(f32[2032]{0:T(1024)} %param.13) | copy-start | bytes 24388
  118.0 23.6 %copy-start.3 = (s32[2032]{0:T(1024)S(1)}, s32[2032]{0:T(1024)}, u32[]{:S(2)}) copy-start(s32[2032]{0:T(1024)} %param.11) | copy-start | bytes 24388
where the time goes:
time: 185 us; the launch traced here: 184 us
  blocking collectives  87.9 us (48%)
  local copies, waits for them, and re-layouts  47.8 us (26%)
  other arithmetic  44 us (24%)
  matrix products  2.74 us (1%)
  between operations  2.08 us (1%)
    unnamed x2, blocking collectives  48.4 us
    gather x1, local copies, waits for them, and re-layouts, body(): passed = jnp.take(date_mask, date_keys, axis=0)  45.5 us
    scatter-add x1, other arithmetic, window_sums(): jax.ops.segment_sum(jnp.where(inside, kept_amount, 0.0), segment, num_seg...  43.2 us
    psum x1, blocking collectives, body(): totals = lax.psum(partial_value, ('rows', 'grp'))  39.5 us

commit v1 on v0

v1 whole, which is shorter than its diff:
```python
import functools

import jax
import jax.numpy as jnp
from jax import lax
from jax.experimental import pallas as pl
from jax.experimental.pallas import tpu as pltpu
from jax.sharding import PartitionSpec as P

CATS = 1000
LANES = 128
MESH = pl.DeviceIdType.MESH
NT = (((1,), (1,)), ((), ()))
SPLITS = 3


def cdiv(a, b):
    return (a + b - 1) // b


def split_bf16(value):
    parts = []
    for _ in range(SPLITS):
        part = value.astype(jnp.bfloat16).astype(jnp.float32)
        parts.append(part)
        value = value - part
    return parts


def divmod_const(keys, size, count):
    block = jnp.zeros_like(keys)
    for step in range(1, count):
        block = block + jnp.where(keys >= step * size, 1, 0)
    return block, keys - block * size


def row(ref, index):
    return ref[pl.ds(index, 1), :]


def kernel(
    rows,
    grps,
    flag_shard,
    shard,
    factor,
    flag_ref,
    table_ref,
    date_ref,
    product_ref,
    quantity_ref,
    out_ref,
    flags,
    tables,
    date_row,
    date_word,
    date_bit,
    key_hi,
    key_lo,
    word,
    kept,
    hist,
    values,
    cat_hi,
    cat_lo,
    grp_sums,
    row_sums,
    send_flag,
    recv_flag,
    send_table,
    recv_table,
    send_grp,
    recv_grp,
    send_row,
    recv_row,
):
    me = lax.axis_index("rows")
    mine = lax.axis_index("grp")
    flag_rows = flag_ref.shape[0]
    table_rows = table_ref.shape[0] // 3
    fact_rows = date_ref.shape[0]
    all_flag_rows = rows * flag_rows
    all_rows = rows * table_rows
    hi_cats = cdiv(CATS, LANES)

    barrier = pltpu.get_barrier_semaphore()
    for step in range(1, rows):
        pl.semaphore_signal(
            barrier, inc=1, device_id=(lax.rem(me + step, rows), mine), device_id_type=MESH
        )
    for step in range(1, grps):
        pl.semaphore_signal(
            barrier, inc=1, device_id=(me, lax.rem(mine + step, grps)), device_id_type=MESH
        )
    pl.semaphore_wait(barrier, rows + grps - 2)

    def to_rows(source, target, send, recv):
        copies = []
        for step in range(1, rows):
            copy = pltpu.make_async_remote_copy(
                src_ref=source,
                dst_ref=target,
                send_sem=send.at[step],
                recv_sem=recv.at[step],
                device_id=(lax.rem(me + step, rows), mine),
                device_id_type=MESH,
            )
            copy.start()
            copies.append(copy)
        return copies

    flag_copies = to_rows(flag_ref, flags.at[me], send_flag, recv_flag)
    table_copies = to_rows(table_ref, tables.at[me], send_table, recv_table)
    flags[pl.ds(me, 1)] = flag_ref[...][None]
    tables[pl.ds(me, 1)] = table_ref[...][None]

    block, inside = divmod_const(date_ref[...], flag_shard, rows)
    date_row[...] = block * flag_rows + inside // LANES
    date_word[...] = (inside % LANES) // 8
    date_bit[...] = inside % 8
    block, inside = divmod_const(product_ref[...], shard, rows)
    key_hi[...] = block * table_rows + inside // LANES
    key_lo[...] = inside % LANES

    for copy in flag_copies:
        copy.wait()

    lane = lax.broadcasted_iota(jnp.int32, (16, LANES), 1)
    place = lax.broadcasted_iota(jnp.int32, (16, LANES), 0)
    weight = jnp.where(
        lane // 8 == place, jnp.left_shift(jnp.ones_like(lane), lane % 8), 0
    ).astype(jnp.float32).astype(jnp.bfloat16)
    words = lax.dot_general(
        weight,
        flags[...].reshape(all_flag_rows, LANES).astype(jnp.bfloat16),
        NT,
        preferred_element_type=jnp.float32,
    ).astype(jnp.bfloat16)
    flag_iota = lax.broadcasted_iota(jnp.int32, (all_flag_rows, LANES), 0)

    @pl.loop(0, fact_rows // 8)
    def _(chunk):
        base = chunk * 8
        onehot = jnp.concatenate(
            [
                jnp.where(flag_iota == row(date_row, base + i), 1.0, 0.0).astype(jnp.bfloat16)
                for i in range(8)
            ],
            axis=1,
        )
        found = jnp.dot(words, onehot, preferred_element_type=jnp.float32)
        for i in range(8):
            piece = found[:, i * LANES : (i + 1) * LANES]
            picked = jnp.where(place == row(date_word, base + i), piece, 0.0)
            word[pl.ds(base + i, 1), :] = jnp.sum(picked, axis=0, keepdims=True)

    passed = jnp.right_shift(word[...].astype(jnp.int32), date_bit[...]) & 1
    for s, part in enumerate(split_bf16(jnp.where(passed == 1, quantity_ref[...], 0.0))):
        kept[s] = part

    square = lax.broadcasted_iota(jnp.int32, (LANES, LANES), 0)
    hist[...] = jnp.zeros_like(hist)

    @pl.loop(0, fact_rows // 8)
    def _(chunk):
        base = chunk * 8
        amounts = [[] for _ in range(SPLITS)]
        for i in range(8):
            mask = square == row(key_lo, base + i)
            for s in range(SPLITS):
                amount = kept[s, pl.ds(base + i, 1), :]
                amounts[s].append(jnp.where(mask, amount, 0.0).astype(jnp.bfloat16))
        amounts = [jnp.concatenate(parts, axis=1) for parts in amounts]

        def add(first, count):
            spot = lax.broadcasted_iota(jnp.int32, (count, LANES), 0) + first
            onehot = jnp.concatenate(
                [
                    jnp.where(spot == row(key_hi, base + i), 1.0, 0.0).astype(jnp.bfloat16)
                    for i in range(8)
                ],
                axis=1,
            )
            total = hist[pl.ds(first, count), :]
            for s in range(SPLITS):
                total = total + lax.dot_general(
                    onehot, amounts[s], NT, preferred_element_type=jnp.float32
                )
            hist[pl.ds(first, count), :] = total

        for first in range(0, all_rows, LANES):
            add(first, min(LANES, all_rows - first))

    for copy in table_copies:
        copy.wait()

    @pl.loop(0, rows)
    def _(r):
        amount = hist[pl.ds(pl.multiple_of(r * table_rows, table_rows), table_rows), :]
        spot = pl.ds(pl.multiple_of(r * table_rows, table_rows), table_rows)
        table = tables[r]
        price = table[:table_rows]
        margin = table[table_rows : 2 * table_rows]
        category = table[2 * table_rows :].astype(jnp.int32)
        cat_hi[spot, :] = category // LANES
        cat_lo[spot, :] = category % LANES
        for s, part in enumerate(split_bf16(amount * price)):
            values[2 * s, spot, :] = part
        for s, part in enumerate(split_bf16(amount * margin)):
            values[2 * s + 1, spot, :] = part

    cat_iota = lax.broadcasted_iota(jnp.int32, (hi_cats, LANES), 0)

    def add_products(chunk, running):
        base = chunk * 8
        lefts, rights = [], []
        for i in range(8):
            mask = cat_iota == row(cat_hi, base + i)
            lefts.append(
                jnp.concatenate(
                    [
                        jnp.where(mask, values[v, pl.ds(base + i, 1), :], 0.0)
                        for v in range(2 * SPLITS)
                    ],
                    axis=0,
                ).astype(jnp.bfloat16)
            )
            rights.append(
                jnp.where(square == row(cat_lo, base + i), 1.0, 0.0).astype(jnp.bfloat16)
            )
        return running + lax.dot_general(
            jnp.concatenate(lefts, axis=1),
            jnp.concatenate(rights, axis=1),
            NT,
            preferred_element_type=jnp.float32,
        )

    summed = lax.fori_loop(
        0,
        all_rows // 8,
        add_products,
        jnp.zeros((2 * SPLITS * hi_cats, LANES), jnp.float32),
    )
    size = 2 * hi_cats
    partial = summed[:size]
    for s in range(1, SPLITS):
        partial = partial + summed[s * size : (s + 1) * size]

    grp_sums[pl.ds(mine, 1)] = partial[None]
    copies = []
    for step in range(1, grps):
        copy = pltpu.make_async_remote_copy(
            src_ref=grp_sums.at[mine],
            dst_ref=grp_sums.at[mine],
            send_sem=send_grp.at[step],
            recv_sem=recv_grp.at[step],
            device_id=(me, lax.rem(mine + step, grps)),
            device_id_type=MESH,
        )
        copy.start()
        copies.append(copy)
    for copy in copies:
        copy.wait()
    total = grp_sums[0]
    for g in range(1, grps):
        total = total + grp_sums[g]

    row_sums[pl.ds(me, 1)] = total[None]
    for copy in to_rows(row_sums.at[me], row_sums.at[me], send_row, recv_row):
        copy.wait()
    total = row_sums[0]
    for r in range(1, rows):
        total = total + row_sums[r]
    out_ref[...] = total * factor


def pad_rows(array, count):
    return jnp.pad(array, (0, count * LANES - array.shape[0])).reshape(count, LANES)


def body(date_keys, product_keys, quantity, date_flags, category, unit_price, unit_cost):
    rows, grps = lax.axis_size("rows"), lax.axis_size("grp")
    facts = date_keys.shape[0]
    shard = unit_price.shape[0]
    flag_shard = date_flags.shape[0]
    flag_rows = cdiv(cdiv(flag_shard, LANES), 8) * 8
    table_rows = cdiv(cdiv(shard, LANES), 8) * 8
    fact_rows = cdiv(facts, 8 * LANES) * 8
    hi_cats = cdiv(CATS, LANES)
    size = 2 * hi_cats
    factor = CATS / (facts * rows * grps)

    flags = pad_rows(jnp.where(date_flags == 1, 1.0, 0.0), flag_rows)
    table = jnp.concatenate(
        [
            pad_rows(unit_price, table_rows),
            pad_rows(unit_price - unit_cost, table_rows),
            pad_rows(category.astype(jnp.float32), table_rows),
        ]
    )
    vmem = pl.BlockSpec(memory_space=pltpu.VMEM)
    ints = pltpu.VMEM((fact_rows, LANES), jnp.int32)
    cat_ints = pltpu.VMEM((rows * table_rows, LANES), jnp.int32)
    out = pl.pallas_call(
        functools.partial(kernel, rows, grps, flag_shard, shard, factor),
        out_shape=jax.ShapeDtypeStruct((size, LANES), jnp.float32),
        in_specs=[vmem] * 5,
        out_specs=vmem,
        scratch_shapes=[
            pltpu.VMEM((rows, flag_rows, LANES), jnp.float32),
            pltpu.VMEM((rows, 3 * table_rows, LANES), jnp.float32),
            ints,
            ints,
            ints,
            ints,
            ints,
            pltpu.VMEM((fact_rows, LANES), jnp.float32),
            pltpu.VMEM((SPLITS, fact_rows, LANES), jnp.float32),
            pltpu.VMEM((rows * table_rows, LANES), jnp.float32),
            pltpu.VMEM((2 * SPLITS, rows * table_rows, LANES), jnp.float32),
            cat_ints,
            cat_ints,
            pltpu.VMEM((grps, size, LANES), jnp.float32),
            pltpu.VMEM((rows, size, LANES), jnp.float32),
        ]
        + [pltpu.SemaphoreType.DMA((rows,))] * 4
        + [pltpu.SemaphoreType.DMA((grps,))] * 2
        + [pltpu.SemaphoreType.DMA((rows,))] * 2,
        compiler_params=pltpu.CompilerParams(collective_id=0, has_side_effects=True),
    )(
        flags,
        table,
        pad_rows(date_keys, fact_rows),
        pad_rows(product_keys, fact_rows),
        pad_rows(quantity, fact_rows),
    )
    return (
        out[:hi_cats].reshape(-1)[:CATS],
        out[hi_cats:].reshape(-1)[:CATS],
    )


def solution(mesh):
    return jax.shard_map(
        body,
        mesh=mesh,
        in_specs=(
            P(("rows", "grp")),
            P(("rows", "grp")),
            P(("rows", "grp")),
            P("rows"),
            P("rows"),
            P("rows"),
            P("rows"),
        ),
        out_specs=(P(), P()),
        check_vma=False,
    )
```

time: 185 us -> 29.7 us (0.16)
  blocking collectives: 87.9 us -> 0 us
  local copies, waits for them, and re-layouts: 47.8 us -> 1.97 us
  other arithmetic: 44 us -> 1.33 us
  Pallas kernels: 0 us -> 25.4 us
  matrix products: 2.74 us -> 0 us
    unnamed x2 -> x0, blocking collectives: 48.4 us -> none
    gather x1 -> x0, local copies, waits for them, and re-layouts: 45.5 us -> none  [body(): passed = jnp.take(date_mask, date_keys, axis=0)]
    scatter-add x1 -> x0, other arithmetic: 43.2 us -> none  [window_sums(): jax.ops.segment_sum(jnp.where(inside, kept_amount, 0.0), segment, num_seg...]
    psum x1 -> x0, blocking collectives: 39.5 us -> none  [body(): totals = lax.psum(partial_value, ('rows', 'grp'))]
    pallas_call x0 -> x1, Pallas kernels: none -> 25.4 us  [body(): pl.pallas_call(functools.partial(kernel, rows, grps, flag_shard, shard, f...]
    dot_general x1 -> x0, matrix products: 2.74 us -> none  [add_block(): jnp.dot(block_amounts, onehot, precision=lax.Precision.HIGHEST, preferred...]
    unnamed x15 -> x6, local copies, waits for them, and re-layouts: 2.26 us -> 0.07 us
    reshape x0 -> x4, local copies, waits for them, and re-layouts: none -> 1.89 us  [the longest x1 1.29 us: body(): return (out[:hi_cats].reshape(-1)[:CATS], out[hi_cats:].reshape(-1)[:CATS])]
where the time goes in v1:
time: 29.7 us; the launch traced here: 29.3 us
  Pallas kernels  25.4 us (86%)
  local copies, waits for them, and re-layouts  1.97 us (7%)
  other arithmetic  1.33 us (4%)
  between operations  0.68 us (2%)
    pallas_call x1, Pallas kernels, body(): pl.pallas_call(functools.partial(kernel, rows, grps, flag_shard, shard, f...  25.4 us
    reshape x1, local copies, waits for them, and re-layouts, body(): return (out[:hi_cats].reshape(-1)[:CATS], out[hi_cats:].reshape(-1)[:CATS])  1.29 us
    convert_element_type x1, other arithmetic, body(): category.astype(jnp.float32)  0.71 us
    concatenate x1, other arithmetic, body(): jnp.concatenate([pad_rows(unit_price, table_rows), pad_rows(unit_price -...  0.61 us
    reshape x3, local copies, waits for them, and re-layouts, pad_rows(): jnp.pad(array, (0, count * LANES - array.shape[0])).reshape(count, LANES)  0.61 us

profile of v1, /device:TPU:0, one launch (start us, length us, event | category | flops | bytes accessed | tf_op | source)
XLA Modules:
  0.0 29.3 jit_solution(17094216455949213598)
XLA Ops:
  0.6 0.0 copy-start
  0.6 0.0 copy-start.1
  0.7 0.7 %convert_element_type.9 = f32[2032]{0:T(1024)S(1)} convert(s32[2032]{0:T(1024)} %param.11) | non-fusion elementwise | flops 2032 | bytes 16256 | tf_op jit(solution)/shard_map/convert_element_type | solution.py:298
  1.4 0.0 copy-done
  1.4 0.0 copy-done.1
  1.4 0.0 copy-start.2
  1.4 0.6 %pad_maximum_fusion.table_ref = f32[48,128]{1,0:T(8,128)} fusion(f32[16,128]{1,0:T(8,128)S(1)} %get-tuple-element.4, f32[16,128]{1,0:T(8,128)S(1)} %get-tuple-element.5, f32[16,128]{1,0:T(8,128)S(1)} %pad_bitcast_fusion.2), kind=kLoop, calls=%fused_computation | loop fusion | flops 12288 | bytes 49152 | tf_op jit(solution)/shard_map/concatenate | solution.py:294
  2.0 0.1 copy-done.2
  2.1 0.6 %pad_bitcast_fusion.3.flag_ref = f32[8,128]{1,0:T(8,128)} fusion(f32[320]{0:T(512)S(1)} %compare_select_fusion), kind=kLoop, calls=%fused_computation.6 | loop fusion | bytes 5376 | tf_op jit(solution)/shard_map/reshape | solution.py:278
  2.7 25.4 %shard_map.86 = f32[16,128]{1,0:T(8,128)} custom-call(f32[8,128]{1,0:T(8,128)} %pad_bitcast_fusion.3.flag_ref, f32[48,128]{1,0:T(8,128)} %pad_maximum_fusion.table_ref, s32[64,128]{1,0:T(8,128)} %bitcast.17, s32[64,128]{1,0:T(8,128)} %bitcast.18, f32[64,128]{1,0:T(8,128)} %bitcast.19), custom_call_target="tpu_custom_call" | custom-call | tf_op jit(solution)/shard_map/pallas_call | solution.py:304
  28.1 1.3 %slice_bitcast_fusion = (f32[1024]{0:T(1024)}, f32[1024]{0:T(1024)}) fusion(f32[16,128]{1,0:T(8,128)} %shard_map.86), kind=kLoop, calls=%fused_computation.4 | loop fusion | bytes 16384 | tf_op jit(solution)/shard_map/reshape | solution.py:339
  (4 shorter events, 0.0 us)
Async XLA Ops:
  0.6 0.7 %copy-start = (f32[2032]{0:T(1024)S(1)}, f32[2032]{0:T(1024)}, u32[]{:S(2)}) copy-start(f32[2032]{0:T(1024)} %param.12) | copy-start | bytes 24388
  0.6 0.7 %copy-start.1 = (f32[2032]{0:T(1024)S(1)}, f32[2032]{0:T(1024)}, u32[]{:S(2)}) copy-start(f32[2032]{0:T(1024)} %param.13) | copy-start | bytes 24388
  1.4 0.7 %copy-start.2 = (s32[320]{0:T(512)S(1)}, s32[320]{0:T(512)}, u32[]{:S(2)}) copy-start(s32[320]{0:T(512)} %param.10) | copy-start | bytes 3844

commit v2 on v1

v2 whole, which is shorter than its diff:
```python
import functools
import math

import jax
import jax.numpy as jnp
from jax import lax
from jax.experimental import pallas as pl
from jax.experimental.pallas import tpu as pltpu
from jax.sharding import PartitionSpec as P

CATS = 1000
LANES = 128
MESH = pl.DeviceIdType.MESH
NT = (((1,), (1,)), ((), ()))
SPLITS = 3


def cdiv(a, b):
    return (a + b - 1) // b


def split_bf16(value):
    parts = []
    for _ in range(SPLITS):
        part = value.astype(jnp.bfloat16).astype(jnp.float32)
        parts.append(part)
        value = value - part
    return parts


def divmod_const(keys, size, count):
    block = jnp.zeros_like(keys)
    for step in range(1, count):
        block = block + jnp.where(keys >= step * size, 1, 0)
    return block, keys - block * size


def packed_row(ref, *index):
    return jnp.broadcast_to(ref[index], (16, LANES)).astype(jnp.bfloat16)


def spots(count):
    shape = (count // 16, 16, LANES)
    tile = lax.broadcasted_iota(jnp.int32, shape, 0)
    line = lax.broadcasted_iota(jnp.int32, shape, 1)
    return (tile * 16 + line).astype(jnp.float32).astype(jnp.bfloat16)


def onehot(numbers, wanted):
    one = jnp.ones_like(numbers)
    hit = jnp.where(numbers == wanted[None], one, jnp.zeros_like(one))
    return hit.reshape(-1, LANES)


def to_dense(target, first, source, length):
    for i in range(cdiv(length, LANES)):
        width = min(LANES, length - i * LANES)
        target[pl.ds(first + i, 1), 0:width] = source(i * LANES, width)


def kernel(
    rows,
    grps,
    factor,
    flag_in,
    category_in,
    price_in,
    cost_in,
    date_in,
    product_in,
    quantity_in,
    out_ref,
    flags,
    flag_rows,
    raw_category,
    raw_price,
    raw_cost,
    tables,
    dates,
    products,
    quantity,
    date_row,
    date_word,
    date_bit,
    key_hi,
    key_lo,
    date_hot,
    hi_hot,
    lo_hot,
    word,
    kept,
    hist,
    values,
    cat_hi,
    cat_lo,
    grp_sums,
    row_sums,
    local,
    send_flag,
    recv_flag,
    send_table,
    recv_table,
    send_grp,
    recv_grp,
    send_row,
    recv_row,
):
    me = lax.axis_index("rows")
    mine = lax.axis_index("grp")
    flag_shard = flag_in.shape[1]
    shard = price_in.shape[1]
    table_rows = tables.shape[1] // 3
    fact_rows = dates.shape[0]
    all_rows = rows * table_rows
    hi_cats = cdiv(CATS, LANES)

    barrier = pltpu.get_barrier_semaphore()
    for step in range(1, rows):
        pl.semaphore_signal(
            barrier, inc=1, device_id=(lax.rem(me + step, rows), mine), device_id_type=MESH
        )
    for step in range(1, grps):
        pl.semaphore_signal(
            barrier, inc=1, device_id=(me, lax.rem(mine + step, grps)), device_id_type=MESH
        )
    inputs = [
        pltpu.make_async_copy(source, target, local.at[i])
        for i, (source, target) in enumerate(
            (
                (flag_in, flags.at[me]),
                (category_in, raw_category),
                (price_in, raw_price),
                (cost_in, raw_cost),
                (product_in, products),
                (date_in, dates),
                (quantity_in, quantity),
            )
        )
    ]
    for copy in inputs:
        copy.start()

    def to_rows(source, target, send, recv):
        copies = []
        for step in range(1, rows):
            copy = pltpu.make_async_remote_copy(
                src_ref=source,
                dst_ref=target,
                send_sem=send.at[step],
                recv_sem=recv.at[step],
                device_id=(lax.rem(me + step, rows), mine),
                device_id_type=MESH,
            )
            copy.start()
            copies.append(copy)
        return copies

    for copy in inputs[:4]:
        copy.wait()
    own = tables.at[me]
    last = cdiv(shard, LANES) - 1
    for i in range(3):
        own[pl.ds(i * table_rows + last, table_rows - last), :] = jnp.zeros(
            (table_rows - last, LANES), jnp.float32
        )
    to_dense(own, 0, lambda at, n: raw_price[:, at : at + n], shard)
    to_dense(
        own, table_rows, lambda at, n: raw_price[:, at : at + n] - raw_cost[:, at : at + n], shard
    )
    to_dense(
        own,
        2 * table_rows,
        lambda at, n: raw_category[:, at : at + n].astype(jnp.float32),
        shard,
    )
    pl.semaphore_wait(barrier, rows + grps - 2)
    flag_copies = to_rows(flags.at[me], flags.at[me], send_flag, recv_flag)
    table_copies = to_rows(tables.at[me], tables.at[me], send_table, recv_table)

    for copy in inputs[4:]:
        copy.wait()
    block, inside = divmod_const(dates[...], flag_shard, rows)
    date_row[...] = (
        block * cdiv(flag_shard, LANES) + jnp.right_shift(inside, 7)
    ).astype(jnp.float32)
    date_word[...] = (jnp.right_shift(inside, 3) & 15).astype(jnp.float32)
    date_bit[...] = inside & 7
    block, inside = divmod_const(products[...], shard, rows)
    key_hi[...] = (block * table_rows + jnp.right_shift(inside, 7)).astype(jnp.float32)
    key_lo[...] = (inside & (LANES - 1)).astype(jnp.float32)
    flag_rows[...] = jnp.zeros_like(flag_rows)
    hist[...] = jnp.zeros_like(hist)
    all_flag_rows = flag_rows.shape[0]

    @pl.loop(0, fact_rows // 8)
    def _(chunk):
        base = chunk * 8
        numbers = spots(LANES)
        for i in range(8):
            line = (pl.ds(base + i, 1), slice(None))
            here = slice(i * LANES, (i + 1) * LANES)
            lo_hot[chunk, :, here] = onehot(numbers, packed_row(key_lo, *line))
            for first in range(0, all_rows, LANES):
                wanted = key_hi[line] - float(first)
                wanted = jnp.broadcast_to(wanted, (16, LANES)).astype(jnp.bfloat16)
                hi_hot[chunk, first : first + LANES, here] = onehot(numbers, wanted)
            for first in range(0, all_flag_rows, LANES):
                count = min(LANES, all_flag_rows - first)
                wanted = date_row[line] - float(first)
                wanted = jnp.broadcast_to(wanted, (16, LANES)).astype(jnp.bfloat16)
                date_hot[chunk, first : first + count, here] = onehot(spots(count), wanted)

    lane = lax.broadcasted_iota(jnp.int32, (16, LANES), 1)
    place = lax.broadcasted_iota(jnp.int32, (16, LANES), 0)
    weight = jnp.where(
        jnp.right_shift(lane, 3) == place, jnp.left_shift(jnp.ones_like(lane), lane & 7), 0
    ).astype(jnp.float32).astype(jnp.bfloat16)
    place = place.astype(jnp.float32)

    for copy in flag_copies:
        copy.wait()
    for r in range(rows):
        to_dense(
            flag_rows,
            r * cdiv(flag_shard, LANES),
            lambda at, n: jnp.where(flags[r, :, at : at + n] == 1, 1.0, 0.0),
            flag_shard,
        )
    words = lax.dot_general(
        weight, flag_rows[...].astype(jnp.bfloat16), NT, preferred_element_type=jnp.float32
    ).astype(jnp.bfloat16)

    @pl.loop(0, fact_rows // 8)
    def _(chunk):
        base = chunk * 8
        found = jnp.dot(words, date_hot[chunk], preferred_element_type=jnp.float32)
        for i in range(8):
            piece = found[:, i * LANES : (i + 1) * LANES]
            picked = jnp.where(place == date_word[pl.ds(base + i, 1), :], piece, 0.0)
            word[pl.ds(base + i, 1), :] = jnp.sum(picked, axis=0, keepdims=True)

    passed = jnp.right_shift(word[...].astype(jnp.int32), date_bit[...]) & 1
    for s, part in enumerate(split_bf16(jnp.where(passed == 1, quantity[...], 0.0))):
        kept[s] = part

    @pl.loop(0, fact_rows // 8)
    def _(chunk):
        base = chunk * 8
        right = lo_hot[chunk]
        amounts = []
        for s in range(SPLITS):
            lines = [packed_row(kept, s, pl.ds(base + i, 1), slice(None)) for i in range(8)]
            amount = jnp.concatenate(lines, axis=1)
            scaled = right.reshape(LANES // 16, 16, 8 * LANES) * amount[None]
            amounts.append(scaled.reshape(LANES, 8 * LANES))
        for first in range(0, all_rows, LANES):
            left = hi_hot[chunk, first : first + LANES, :]
            total = hist[pl.ds(first, LANES), :]
            for s in range(SPLITS):
                total = total + lax.dot_general(
                    left, amounts[s], NT, preferred_element_type=jnp.float32
                )
            hist[pl.ds(first, LANES), :] = total

    for copy in table_copies:
        copy.wait()

    @pl.loop(0, rows)
    def _(r):
        spot = pl.ds(pl.multiple_of(r * table_rows, table_rows), table_rows)
        amount = hist[spot, :]
        table = tables[r]
        category = table[2 * table_rows :].astype(jnp.int32)
        cat_hi[spot, :] = jnp.right_shift(category, 7).astype(jnp.float32)
        cat_lo[spot, :] = (category & (LANES - 1)).astype(jnp.float32)
        for s, part in enumerate(split_bf16(amount * table[:table_rows])):
            values[2 * s, spot, :] = part
        for s, part in enumerate(split_bf16(amount * table[table_rows : 2 * table_rows])):
            values[2 * s + 1, spot, :] = part

    cat_iota = lax.broadcasted_iota(jnp.int32, (hi_cats, LANES), 0).astype(jnp.float32)

    def add_products(chunk, running):
        base = chunk * 8
        numbers = spots(LANES)
        lefts, rights = [], []
        for i in range(8):
            line = (pl.ds(base + i, 1), slice(None))
            mask = cat_iota == cat_hi[line]
            lefts.append(
                jnp.concatenate(
                    [jnp.where(mask, values[v, line[0], :], 0.0) for v in range(2 * SPLITS)],
                    axis=0,
                ).astype(jnp.bfloat16)
            )
            rights.append(onehot(numbers, packed_row(cat_lo, *line)))
        return running + lax.dot_general(
            jnp.concatenate(lefts, axis=1),
            jnp.concatenate(rights, axis=1),
            NT,
            preferred_element_type=jnp.float32,
        )

    summed = lax.fori_loop(
        0,
        all_rows // 8,
        add_products,
        jnp.zeros((2 * SPLITS * hi_cats, LANES), jnp.float32),
    )
    size = 2 * hi_cats
    partial = summed[:size]
    for s in range(1, SPLITS):
        partial = partial + summed[s * size : (s + 1) * size]

    grp_sums[pl.ds(mine, 1)] = partial[None]
    copies = []
    for step in range(1, grps):
        copy = pltpu.make_async_remote_copy(
            src_ref=grp_sums.at[mine],
            dst_ref=grp_sums.at[mine],
            send_sem=send_grp.at[step],
            recv_sem=recv_grp.at[step],
            device_id=(me, lax.rem(mine + step, grps)),
            device_id_type=MESH,
        )
        copy.start()
        copies.append(copy)
    for copy in copies:
        copy.wait_recv()
    total = grp_sums[0]
    for g in range(1, grps):
        total = total + grp_sums[g]

    row_sums[pl.ds(me, 1)] = total[None]
    last_copies = to_rows(row_sums.at[me], row_sums.at[me], send_row, recv_row)
    for copy in copies:
        copy.wait_send()
    for copy in last_copies:
        copy.wait()
    total = row_sums[0]
    for r in range(1, rows):
        total = total + row_sums[r]
    out_ref[...] = total * factor


def body(date_keys, product_keys, quantity, date_flags, category, unit_price, unit_cost):
    rows, grps = lax.axis_size("rows"), lax.axis_size("grp")
    facts = date_keys.shape[0]
    shard = unit_price.shape[0]
    flag_shard = date_flags.shape[0]
    table_rows = cdiv(cdiv(shard, LANES), 16) * 16
    fact_rows = cdiv(facts, 8 * LANES) * 8
    chunks = fact_rows // 8
    all_rows = cdiv(rows * table_rows, LANES) * LANES
    all_flag_rows = cdiv(rows * cdiv(flag_shard, LANES), 16) * 16
    hi_cats = cdiv(CATS, LANES)
    size = 2 * hi_cats
    factor = CATS / (facts * rows * grps)

    def by_rows(array):
        return jnp.pad(array, (0, fact_rows * LANES - facts)).reshape(fact_rows, LANES)

    f32, i32, bf16 = jnp.float32, jnp.int32, jnp.bfloat16
    dense = (fact_rows, LANES)
    scratch = [
        ((rows, 1, flag_shard), i32),
        ((all_flag_rows, LANES), f32),
        ((1, shard), i32),
        ((1, shard), f32),
        ((1, shard), f32),
        ((rows, 3 * table_rows, LANES), f32),
        (dense, i32),
        (dense, i32),
        (dense, f32),
        (dense, f32),
        (dense, f32),
        (dense, i32),
        (dense, f32),
        (dense, f32),
        ((chunks, all_flag_rows, 8 * LANES), bf16),
        ((chunks, all_rows, 8 * LANES), bf16),
        ((chunks, LANES, 8 * LANES), bf16),
        (dense, f32),
        ((SPLITS,) + dense, f32),
        ((all_rows, LANES), f32),
        ((2 * SPLITS, all_rows, LANES), f32),
        ((all_rows, LANES), f32),
        ((all_rows, LANES), f32),
        ((grps, size, LANES), f32),
        ((rows, size, LANES), f32),
    ]
    bytes_held = sum(math.prod(shape) * jnp.dtype(kind).itemsize for shape, kind in scratch)
    out = pl.pallas_call(
        functools.partial(kernel, rows, grps, factor),
        out_shape=jax.ShapeDtypeStruct((size, LANES), f32),
        in_specs=[pl.BlockSpec(memory_space=pl.ANY)] * 7,
        out_specs=pl.BlockSpec(memory_space=pltpu.VMEM),
        scratch_shapes=[pltpu.VMEM(shape, kind) for shape, kind in scratch]
        + [pltpu.SemaphoreType.DMA((7,))]
        + [pltpu.SemaphoreType.DMA((rows,))] * 4
        + [pltpu.SemaphoreType.DMA((grps,))] * 2
        + [pltpu.SemaphoreType.DMA((rows,))] * 2,
        compiler_params=pltpu.CompilerParams(
            collective_id=0,
            has_side_effects=True,
            vmem_limit_bytes=2 * bytes_held + (8 << 20),
        ),
    )(
        date_flags.reshape(1, -1),
        category.reshape(1, -1),
        unit_price.reshape(1, -1),
        unit_cost.reshape(1, -1),
        by_rows(date_keys),
        by_rows(product_keys),
        by_rows(quantity),
    )
    return (
        out[:hi_cats].reshape(-1)[:CATS],
        out[hi_cats:].reshape(-1)[:CATS],
    )


def solution(mesh):
    return jax.shard_map(
        body,
        mesh=mesh,
        in_specs=(
            P(("rows", "grp")),
            P(("rows", "grp")),
            P(("rows", "grp")),
            P("rows"),
            P("rows"),
            P("rows"),
            P("rows"),
        ),
        out_specs=(P(), P()),
        check_vma=False,
    )
```

time: 29.7 us -> 29.7 us (level)
  local copies, waits for them, and re-layouts: 1.97 us -> 4.95 us
  Pallas kernels: 25.4 us -> 23.6 us
  other arithmetic: 1.33 us -> 0 us
    unnamed x6 -> x14, local copies, waits for them, and re-layouts: 0.07 us -> 4.35 us
    pallas_call x1, Pallas kernels: 25.4 us -> 23.6 us  [body(): pl.pallas_call(functools.partial(kernel, rows, grps, factor), out_shape=j...]
    convert_element_type x1 -> x0, other arithmetic: 0.71 us -> none  [body(): category.astype(jnp.float32)]
    reshape x1, local copies, waits for them, and re-layouts: 1.29 us -> 0.6 us  [body(): return (out[:hi_cats].reshape(-1)[:CATS], out[hi_cats:].reshape(-1)[:CATS])]
    concatenate x1 -> x0, other arithmetic: 0.61 us -> none  [body(): jnp.concatenate([pad_rows(unit_price, table_rows), pad_rows(unit_price -...]
    reshape x3 -> x1, local copies, waits for them, and re-layouts: 0.61 us -> 0.01 us  [body(): date_flags.reshape(1, -1)]
where the time goes in v2:
time: 29.7 us; the launch traced here: 29.2 us
  Pallas kernels  23.6 us (79%)
  local copies, waits for them, and re-layouts  4.95 us (17%)
  between operations  0.66 us (2%)
    pallas_call x1, Pallas kernels, body(): pl.pallas_call(functools.partial(kernel, rows, grps, factor), out_shape=j...  23.6 us
    unnamed x14, local copies, waits for them, and re-layouts  4.35 us
    reshape x1, local copies, waits for them, and re-layouts, body(): return (out[:hi_cats].reshape(-1)[:CATS], out[hi_cats:].reshape(-1)[:CATS])  0.6 us

profile of v2, /device:TPU:0, one launch (start us, length us, event | category | flops | bytes accessed | tf_op | source)
XLA Modules:
  0.0 29.2 jit_solution(15416884611312527200)
XLA Ops:
  0.6 0.0 copy-start.3
  0.6 0.0 copy-start.6
  0.6 0.7 %copy-done.6 = s32[320]{0:T(512)S(1)} copy-done((s32[320]{0:T(512)S(1)}, s32[320]{0:T(512)}, u32[]{:S(2)}) %copy-start.6) | copy-done | bytes 1304
  1.3 0.0 copy-done.3
  1.3 0.0 copy-start
  1.3 0.8 %copy-done = s32[8192]{0:T(1024)S(1)} copy-done((s32[8192]{0:T(1024)S(1)}, s32[8192]{0:T(1024)}, u32[]{:S(2)}) %copy-start) | copy-done | bytes 32792
  2.1 0.0 copy-start.1
  2.1 0.8 %copy-done.1 = s32[8192]{0:T(1024)S(1)} copy-done((s32[8192]{0:T(1024)S(1)}, s32[8192]{0:T(1024)}, u32[]{:S(2)}) %copy-start.1) | copy-done | bytes 32792
  2.9 0.0 copy-start.2
  2.9 0.8 %copy-done.2 = f32[8192]{0:T(1024)S(1)} copy-done((f32[8192]{0:T(1024)S(1)}, f32[8192]{0:T(1024)}, u32[]{:S(2)}) %copy-start.2) | copy-done | bytes 32792
  3.6 0.0 copy-start.4
  3.6 0.7 %copy-done.4 = f32[2032]{0:T(1024)S(1)} copy-done((f32[2032]{0:T(1024)S(1)}, f32[2032]{0:T(1024)}, u32[]{:S(2)}) %copy-start.4) | copy-done | bytes 8152
  4.3 0.0 copy-start.5
  4.3 0.7 %copy-done.5 = f32[2032]{0:T(1024)S(1)} copy-done((f32[2032]{0:T(1024)S(1)}, f32[2032]{0:T(1024)}, u32[]{:S(2)}) %copy-start.5) | copy-done | bytes 8152
  5.0 23.6 %shard_map.86 = f32[16,128]{1,0:T(8,128)S(1)} custom-call(s32[1,320]{1,0:T(1,128)S(1)} %reshape.31.flag_in, s32[1,2032]{1,0:T(1,128)S(1)} %bitcast.15, f32[1,2032]{1,0:T(1,128)S(1)} %bitcast.16, f32[1,2032]{1,0:T(1,128)S(1)} %bitcast.17, s32[64,128]{1,0:T(8,128)S(1)} %bitcast.12, s32[64,128]{1,0:T(8,128)S(1)} %bitcast.13, f32[64,128]{1,0:T(8,128)S(1)} %bitcast.14), custom_call_target="tpu_custom_call" | custom-call | tf_op jit(solution)/shard_map/pallas_call | solution.py:393
  28.6 0.6 %slice_bitcast_fusion = (f32[1024]{0:T(1024)}, f32[1024]{0:T(1024)}) fusion(f32[16,128]{1,0:T(8,128)S(1)} %shard_map.86), kind=kLoop, calls=%fused_computation | loop fusion | bytes 16384 | tf_op jit(solution)/shard_map/reshape | solution.py:419
  (1 shorter events, 0.0 us)
Async XLA Ops:
  0.6 0.7 %copy-start.3 = (s32[2032]{0:T(1024)S(1)}, s32[2032]{0:T(1024)}, u32[]{:S(2)}) copy-start(s32[2032]{0:T(1024)} %param.11) | copy-start | bytes 24388
  0.6 0.7 %copy-start.6 = (s32[320]{0:T(512)S(1)}, s32[320]{0:T(512)}, u32[]{:S(2)}) copy-start(s32[320]{0:T(512)} %param.10) | copy-start | bytes 3844
  1.3 0.8 %copy-start = (s32[8192]{0:T(1024)S(1)}, s32[8192]{0:T(1024)}, u32[]{:S(2)}) copy-start(s32[8192]{0:T(1024)} %param.7) | copy-start | bytes 98308
  2.1 0.8 %copy-start.1 = (s32[8192]{0:T(1024)S(1)}, s32[8192]{0:T(1024)}, u32[]{:S(2)}) copy-start(s32[8192]{0:T(1024)} %param.8) | copy-start | bytes 98308
  2.9 0.8 %copy-start.2 = (f32[8192]{0:T(1024)S(1)}, f32[8192]{0:T(1024)}, u32[]{:S(2)}) copy-start(f32[8192]{0:T(1024)} %param.9) | copy-start | bytes 98308
  3.6 0.7 %copy-start.4 = (f32[2032]{0:T(1024)S(1)}, f32[2032]{0:T(1024)}, u32[]{:S(2)}) copy-start(f32[2032]{0:T(1024)} %param.12) | copy-start | bytes 24388
  4.3 0.7 %copy-start.5 = (f32[2032]{0:T(1024)S(1)}, f32[2032]{0:T(1024)}, u32[]{:S(2)}) copy-start(f32[2032]{0:T(1024)} %param.13) | copy-start | bytes 24388

commit v3 on v2

--- a/solution.py
+++ b/solution.py
@@ -1,5 +1,4 @@
 import functools
-import math
 
 import jax
 import jax.numpy as jnp
@@ -107,7 +106,7 @@
 ):
     me = lax.axis_index("rows")
     mine = lax.axis_index("grp")
-    flag_shard = flag_in.shape[1]
+    flag_shard = flag_in.shape[0]
     shard = price_in.shape[1]
     table_rows = tables.shape[1] // 3
     fact_rows = dates.shape[0]
@@ -127,7 +126,7 @@
         pltpu.make_async_copy(source, target, local.at[i])
         for i, (source, target) in enumerate(
             (
-                (flag_in, flags.at[me]),
+                (flag_in, flags.at[me, 0]),
                 (category_in, raw_category),
                 (price_in, raw_price),
                 (cost_in, raw_cost),
@@ -389,11 +388,10 @@
         ((grps, size, LANES), f32),
         ((rows, size, LANES), f32),
     ]
-    bytes_held = sum(math.prod(shape) * jnp.dtype(kind).itemsize for shape, kind in scratch)
     out = pl.pallas_call(
         functools.partial(kernel, rows, grps, factor),
         out_shape=jax.ShapeDtypeStruct((size, LANES), f32),
-        in_specs=[pl.BlockSpec(memory_space=pl.ANY)] * 7,
+        in_specs=[pl.BlockSpec(memory_space=pltpu.HBM)] * 7,
         out_specs=pl.BlockSpec(memory_space=pltpu.VMEM),
         scratch_shapes=[pltpu.VMEM(shape, kind) for shape, kind in scratch]
         + [pltpu.SemaphoreType.DMA((7,))]
@@ -403,10 +401,9 @@
         compiler_params=pltpu.CompilerParams(
             collective_id=0,
             has_side_effects=True,
-            vmem_limit_bytes=2 * bytes_held + (8 << 20),
         ),
     )(
-        date_flags.reshape(1, -1),
+        date_flags,
         category.reshape(1, -1),
         unit_price.reshape(1, -1),
         unit_cost.reshape(1, -1),

time: 29.7 us -> 26.4 us (0.89)
  local copies, waits for them, and re-layouts: 4.95 us -> 1.28 us
  Pallas kernels: 23.6 us -> 24.2 us
    unnamed x14 -> x0, local copies, waits for them, and re-layouts: 4.35 us -> none
    reshape x1, local copies, waits for them, and re-layouts: 0.6 us -> 1.28 us  [body(): return (out[:hi_cats].reshape(-1)[:CATS], out[hi_cats:].reshape(-1)[:CATS])]
    pallas_call x1, Pallas kernels: 23.6 us -> 24.2 us  [body(): pl.pallas_call(functools.partial(kernel, rows, grps, factor), out_shape=j...]
where the time goes in v3:
time: 26.4 us; the launch traced here: 26.1 us
  Pallas kernels  24.2 us (92%)
  local copies, waits for them, and re-layouts  1.28 us (5%)
  between operations  0.64 us (2%)
    pallas_call x1, Pallas kernels, body(): pl.pallas_call(functools.partial(kernel, rows, grps, factor), out_shape=j...  24.2 us
    reshape x1, local copies, waits for them, and re-layouts, body(): return (out[:hi_cats].reshape(-1)[:CATS], out[hi_cats:].reshape(-1)[:CATS])  1.28 us

profile of v3, /device:TPU:0, one launch (start us, length us, event | category | flops | bytes accessed | tf_op | source)
XLA Modules:
  0.0 26.1 jit_solution(9194656972283302939)
XLA Ops:
  0.6 24.2 %shard_map.86 = f32[16,128]{1,0:T(8,128)} custom-call(s32[320]{0:T(512)} %flag_in.1, s32[1,2032]{1,0:T(1,128)} %bitcast.15, f32[1,2032]{1,0:T(1,128)} %bitcast.16, f32[1,2032]{1,0:T(1,128)} %bitcast.17, s32[64,128]{1,0:T(8,128)} %bitcast.12, s32[64,128]{1,0:T(8,128)} %bitcast.13, f32[64,128]{1,0:T(8,128)} %bitcast.14), custom_call_target="tpu_custom_call" | custom-call | tf_op jit(solution)/shard_map/pallas_call | solution.py:391
  24.9 1.3 %slice_bitcast_fusion = (f32[1024]{0:T(1024)}, f32[1024]{0:T(1024)}) fusion(f32[16,128]{1,0:T(8,128)} %shard_map.86), kind=kLoop, calls=%fused_computation | loop fusion | bytes 16384 | tf_op jit(solution)/shard_map/reshape | solution.py:416

commit v4 on v3

--- a/solution.py
+++ b/solution.py
@@ -12,6 +12,8 @@
 MESH = pl.DeviceIdType.MESH
 NT = (((1,), (1,)), ((), ()))
 SPLITS = 3
+STEP = 32
+FACT_STEP = 32
 
 
 def cdiv(a, b):
@@ -39,16 +41,15 @@
 
 
 def spots(count):
-    shape = (count // 16, 16, LANES)
-    tile = lax.broadcasted_iota(jnp.int32, shape, 0)
-    line = lax.broadcasted_iota(jnp.int32, shape, 1)
-    return (tile * 16 + line).astype(jnp.float32).astype(jnp.bfloat16)
-
-
-def onehot(numbers, wanted):
-    one = jnp.ones_like(numbers)
-    hit = jnp.where(numbers == wanted[None], one, jnp.zeros_like(one))
-    return hit.reshape(-1, LANES)
+    line = lax.broadcasted_iota(jnp.int32, (16, LANES), 0).astype(jnp.float32)
+    return [(line + float(first)).astype(jnp.bfloat16) for first in range(0, count, 16)]
+
+
+def marked(numbers, wanted, amount):
+    zero = jnp.zeros_like(wanted)
+    return jnp.concatenate(
+        [jnp.where(tile == wanted, amount, zero) for tile in numbers], axis=0
+    )
 
 
 def to_dense(target, first, source, length):
@@ -83,9 +84,6 @@
     date_bit,
     key_hi,
     key_lo,
-    date_hot,
-    hi_hot,
-    lo_hot,
     word,
     kept,
     hist,
@@ -185,29 +183,13 @@
     date_word[...] = (jnp.right_shift(inside, 3) & 15).astype(jnp.float32)
     date_bit[...] = inside & 7
     block, inside = divmod_const(products[...], shard, rows)
-    key_hi[...] = (block * table_rows + jnp.right_shift(inside, 7)).astype(jnp.float32)
-    key_lo[...] = (inside & (LANES - 1)).astype(jnp.float32)
+    line = block * table_rows + jnp.right_shift(inside, 7)
+    half = jnp.right_shift(line, 6) & 1
+    key_hi[...] = (jnp.right_shift(line, 7) * 64 + (line & 63)).astype(jnp.float32)
+    key_lo[...] = ((inside & (LANES - 1)) + half * LANES).astype(jnp.float32)
     flag_rows[...] = jnp.zeros_like(flag_rows)
     hist[...] = jnp.zeros_like(hist)
     all_flag_rows = flag_rows.shape[0]
-
-    @pl.loop(0, fact_rows // 8)
-    def _(chunk):
-        base = chunk * 8
-        numbers = spots(LANES)
-        for i in range(8):
-            line = (pl.ds(base + i, 1), slice(None))
-            here = slice(i * LANES, (i + 1) * LANES)
-            lo_hot[chunk, :, here] = onehot(numbers, packed_row(key_lo, *line))
-            for first in range(0, all_rows, LANES):
-                wanted = key_hi[line] - float(first)
-                wanted = jnp.broadcast_to(wanted, (16, LANES)).astype(jnp.bfloat16)
-                hi_hot[chunk, first : first + LANES, here] = onehot(numbers, wanted)
-            for first in range(0, all_flag_rows, LANES):
-                count = min(LANES, all_flag_rows - first)
-                wanted = date_row[line] - float(first)
-                wanted = jnp.broadcast_to(wanted, (16, LANES)).astype(jnp.bfloat16)
-                date_hot[chunk, first : first + count, here] = onehot(spots(count), wanted)
 
     lane = lax.broadcasted_iota(jnp.int32, (16, LANES), 1)
     place = lax.broadcasted_iota(jnp.int32, (16, LANES), 0)
@@ -229,11 +211,16 @@
         weight, flag_rows[...].astype(jnp.bfloat16), NT, preferred_element_type=jnp.float32
     ).astype(jnp.bfloat16)
 
-    @pl.loop(0, fact_rows // 8)
+    @pl.loop(0, fact_rows // FACT_STEP)
     def _(chunk):
-        base = chunk * 8
-        found = jnp.dot(words, date_hot[chunk], preferred_element_type=jnp.float32)
-        for i in range(8):
+        base = chunk * FACT_STEP
+        numbers = spots(all_flag_rows)
+        lines = [packed_row(date_row, pl.ds(base + i, 1), slice(None)) for i in range(FACT_STEP)]
+        hot = jnp.concatenate(
+            [marked(numbers, line, jnp.ones_like(line)) for line in lines], axis=1
+        )
+        found = jnp.dot(words, hot, preferred_element_type=jnp.float32)
+        for i in range(FACT_STEP):
             piece = found[:, i * LANES : (i + 1) * LANES]
             picked = jnp.where(place == date_word[pl.ds(base + i, 1), :], piece, 0.0)
             word[pl.ds(base + i, 1), :] = jnp.sum(picked, axis=0, keepdims=True)
@@ -242,24 +229,34 @@
     for s, part in enumerate(split_bf16(jnp.where(passed == 1, quantity[...], 0.0))):
         kept[s] = part
 
-    @pl.loop(0, fact_rows // 8)
+    @pl.loop(0, fact_rows // FACT_STEP)
     def _(chunk):
-        base = chunk * 8
-        right = lo_hot[chunk]
-        amounts = []
-        for s in range(SPLITS):
-            lines = [packed_row(kept, s, pl.ds(base + i, 1), slice(None)) for i in range(8)]
-            amount = jnp.concatenate(lines, axis=1)
-            scaled = right.reshape(LANES // 16, 16, 8 * LANES) * amount[None]
-            amounts.append(scaled.reshape(LANES, 8 * LANES))
+        base = chunk * FACT_STEP
+        numbers, row_numbers = spots(2 * LANES), spots(64)
+        lows = [packed_row(key_lo, pl.ds(base + i, 1), slice(None)) for i in range(FACT_STEP)]
+        right = jnp.concatenate([marked(numbers, low, jnp.ones_like(low)) for low in lows], axis=1)
+        amounts = [
+            [packed_row(kept, s, pl.ds(base + i, 1), slice(None)) for s in range(SPLITS)]
+            for i in range(FACT_STEP)
+        ]
         for first in range(0, all_rows, LANES):
-            left = hi_hot[chunk, first : first + LANES, :]
-            total = hist[pl.ds(first, LANES), :]
-            for s in range(SPLITS):
-                total = total + lax.dot_general(
-                    left, amounts[s], NT, preferred_element_type=jnp.float32
+            lefts = []
+            for i in range(FACT_STEP):
+                wanted = jnp.broadcast_to(key_hi[pl.ds(base + i, 1), :] - float(first // 2), (16, LANES))
+                wanted = wanted.astype(jnp.bfloat16)
+                lefts.append(
+                    jnp.concatenate(
+                        [marked(row_numbers, wanted, amount) for amount in amounts[i]], axis=0
+                    )
                 )
-            hist[pl.ds(first, LANES), :] = total
+            summed = lax.dot_general(
+                jnp.concatenate(lefts, axis=1), right, NT, preferred_element_type=jnp.float32
+            )
+            total = summed[:64]
+            for s in range(1, SPLITS):
+                total = total + summed[s * 64 : (s + 1) * 64]
+            hist[pl.ds(first, 64), :] += total[:, :LANES]
+            hist[pl.ds(first + 64, 64), :] += total[:, LANES:]
 
     for copy in table_copies:
         copy.wait()
@@ -270,46 +267,57 @@
         amount = hist[spot, :]
         table = tables[r]
         category = table[2 * table_rows :].astype(jnp.int32)
-        cat_hi[spot, :] = jnp.right_shift(category, 7).astype(jnp.float32)
-        cat_lo[spot, :] = (category & (LANES - 1)).astype(jnp.float32)
+        half = jnp.right_shift(category, 6) & 1
+        cat_hi[spot, :] = (jnp.right_shift(category, 7) + half * hi_cats).astype(jnp.float32)
+        cat_lo[spot, :] = (category & (LANES // 2 - 1)).astype(jnp.float32)
         for s, part in enumerate(split_bf16(amount * table[:table_rows])):
             values[2 * s, spot, :] = part
         for s, part in enumerate(split_bf16(amount * table[table_rows : 2 * table_rows])):
             values[2 * s + 1, spot, :] = part
 
-    cat_iota = lax.broadcasted_iota(jnp.int32, (hi_cats, LANES), 0).astype(jnp.float32)
+    halves = cdiv(2 * hi_cats, 16) * 16
 
     def add_products(chunk, running):
-        base = chunk * 8
-        numbers = spots(LANES)
+        base = chunk * STEP
+        row_numbers, numbers = spots(halves), spots(LANES // 2)
         lefts, rights = [], []
-        for i in range(8):
+        for i in range(STEP):
             line = (pl.ds(base + i, 1), slice(None))
-            mask = cat_iota == cat_hi[line]
+            wanted = packed_row(cat_hi, *line)
             lefts.append(
                 jnp.concatenate(
-                    [jnp.where(mask, values[v, line[0], :], 0.0) for v in range(2 * SPLITS)],
+                    [
+                        marked(row_numbers, wanted, packed_row(values, v, *line))
+                        for v in range(2 * SPLITS)
+                    ],
                     axis=0,
-                ).astype(jnp.bfloat16)
+                )
             )
-            rights.append(onehot(numbers, packed_row(cat_lo, *line)))
-        return running + lax.dot_general(
+            low = packed_row(cat_lo, *line)
+            rights.append(marked(numbers, low, jnp.ones_like(low)))
+        summed = lax.dot_general(
             jnp.concatenate(lefts, axis=1),
             jnp.concatenate(rights, axis=1),
             NT,
             preferred_element_type=jnp.float32,
         )
+        for s in range(SPLITS):
+            running = running + summed[2 * s * halves : 2 * (s + 1) * halves]
+        return running
 
     summed = lax.fori_loop(
         0,
-        all_rows // 8,
+        all_rows // STEP,
         add_products,
-        jnp.zeros((2 * SPLITS * hi_cats, LANES), jnp.float32),
-    )
-    size = 2 * hi_cats
-    partial = summed[:size]
-    for s in range(1, SPLITS):
-        partial = partial + summed[s * size : (s + 1) * size]
+        jnp.zeros((2 * halves, LANES // 2), jnp.float32),
+    )
+    outputs = []
+    for v in range(2):
+        whole = summed[v * halves : (v + 1) * halves]
+        outputs.append(
+            jnp.concatenate([whole[:hi_cats], whole[hi_cats : 2 * hi_cats]], axis=1)
+        )
+    partial = jnp.concatenate(outputs, axis=0)
 
     grp_sums[pl.ds(mine, 1)] = partial[None]
     copies = []
@@ -348,8 +356,7 @@
     shard = unit_price.shape[0]
     flag_shard = date_flags.shape[0]
     table_rows = cdiv(cdiv(shard, LANES), 16) * 16
-    fact_rows = cdiv(facts, 8 * LANES) * 8
-    chunks = fact_rows // 8
+    fact_rows = cdiv(facts, 32 * LANES) * 32
     all_rows = cdiv(rows * table_rows, LANES) * LANES
     all_flag_rows = cdiv(rows * cdiv(flag_shard, LANES), 16) * 16
     hi_cats = cdiv(CATS, LANES)
@@ -359,7 +366,7 @@
     def by_rows(array):
         return jnp.pad(array, (0, fact_rows * LANES - facts)).reshape(fact_rows, LANES)
 
-    f32, i32, bf16 = jnp.float32, jnp.int32, jnp.bfloat16
+    f32, i32 = jnp.float32, jnp.int32
     dense = (fact_rows, LANES)
     scratch = [
         ((rows, 1, flag_shard), i32),
@@ -376,9 +383,6 @@
         (dense, i32),
         (dense, f32),
         (dense, f32),
-        ((chunks, all_flag_rows, 8 * LANES), bf16),
-        ((chunks, all_rows, 8 * LANES), bf16),
-        ((chunks, LANES, 8 * LANES), bf16),
         (dense, f32),
         ((SPLITS,) + dense, f32),
         ((all_rows, LANES), f32),

time: 26.4 us -> 22.6 us (0.86)
  Pallas kernels: 24.2 us -> 20.4 us
    pallas_call x1, Pallas kernels: 24.2 us -> 20.4 us  [body(): pl.pallas_call(functools.partial(kernel, rows, grps, factor), out_shape=j...]
where the time goes in v4:
time: 22.6 us; the launch traced here: 22.4 us
  Pallas kernels  20.4 us (90%)
  local copies, waits for them, and re-layouts  1.28 us (6%)
  between operations  0.64 us (3%)
    pallas_call x1, Pallas kernels, body(): pl.pallas_call(functools.partial(kernel, rows, grps, factor), out_shape=j...  20.4 us
    reshape x1, local copies, waits for them, and re-layouts, body(): return (out[:hi_cats].reshape(-1)[:CATS], out[hi_cats:].reshape(-1)[:CATS])  1.28 us

profile of v4, /device:TPU:0, one launch (start us, length us, event | category | flops | bytes accessed | tf_op | source)
XLA Modules:
  0.0 22.4 jit_solution(1226891522303300705)
XLA Ops:
  0.6 20.4 %shard_map.86 = f32[16,128]{1,0:T(8,128)} custom-call(s32[320]{0:T(512)} %flag_in.1, s32[1,2032]{1,0:T(1,128)} %bitcast.15, f32[1,2032]{1,0:T(1,128)} %bitcast.16, f32[1,2032]{1,0:T(1,128)} %bitcast.17, s32[64,128]{1,0:T(8,128)} %bitcast.12, s32[64,128]{1,0:T(8,128)} %bitcast.13, f32[64,128]{1,0:T(8,128)} %bitcast.14), custom_call_target="tpu_custom_call" | custom-call | tf_op jit(solution)/shard_map/pallas_call | solution.py:395
  21.1 1.3 %slice_bitcast_fusion = (f32[1024]{0:T(1024)}, f32[1024]{0:T(1024)}) fusion(f32[16,128]{1,0:T(8,128)} %shard_map.86), kind=kLoop, calls=%fused_computation | loop fusion | bytes 16384 | tf_op jit(solution)/shard_map/reshape | solution.py:420
